TPU v7x, 512 devices: a whole 4x8x8 slice. The times are simulated.
512 devices in a mesh: slab: 128 (over z, x, y_lo), sec: 4 (over y_hi, core).
Axes of the slice: x: 4, y: 8 (y_hi: 2, y_lo: 4; y = y_hi * 4 + y_lo), z: 8, core: 2. Of those that a mesh axis runs over, the one named last changes fastest.
Arguments:
- displacement: float32 [5120, 4096], P('slab', 'sec'), may hold values from -6 to 6
- earlier_field: float32 [5120, 4096], P('slab', 'sec'), may hold values from -6 to 6
- region_ids: int32 [4096], P('sec'), may hold values from 0 to 7
- material: float32 [2, 8], replicated, may hold values from 0.5 to 1.5
- mode_shapes: float32 [4096, 64], P('sec'), may hold values from -0.75 to 0.75
- band_edges: int32 [2, 64], replicated, may hold values from 0 to 4095, as said below
Outputs:
- advanced_field: float32 [5120, 4096], P('slab', 'sec')
- band_field: bfloat16 [5120, 4096], P('slab', 'sec')
Inputs may be any that keep to these rules, and one draw needn't show every extreme that they name: `band_edges`: for every mode the lower edge is below the upper edge; some mode's band starts at 0 and some mode's band ends at 4095.
All inputs are finite; a program needn't handle non-finite values.
Results may differ from a plain program's by a relative error of at most 0.001.
Values sent between devices are 32-bit elements; how exact they have to be, the bound alone decides.
A program may use at most 64 MiB of HBM per device.

v0:
```python
import math
import jax
import jax.numpy as jnp
from jax import lax
from jax.sharding import PartitionSpec as P

COLS = 64
MODES = 64
WAVES = 4096
REGIONS = 8
STEPS = 4
courant_sq = 0.14
two_pi = 2.0 * math.pi


def extended_2(x, sides, width, wrap):
    for axis, dim in sides:
        peers, length = (lax.axis_size(axis), x.shape[dim])
        up = [(i, (i + 1) % peers) for i in range(peers if wrap else peers - 1)]
        down = [(j, i) for i, j in up]
        last = lax.slice_in_dim(x, length - width, length, axis=dim)
        leading = lax.slice_in_dim(x, 0, width, axis=dim)
        before = lax.ppermute(last, axis, up)
        after = lax.ppermute(leading, axis, down)
        x = jnp.concatenate([before, x, after], axis=dim)
    return x


def lookup_stiffness(region_ids, material):
    values = courant_sq * material[0] * material[1]
    match = region_ids[:, None] == jnp.arange(REGIONS, dtype=jnp.int32)[None, :]
    return jnp.sum(jnp.where(match, values[None, :], jnp.zeros_like(values)[None, :]), axis=1)


def advance(extended, before, stiffness):
    centre = extended[1:-1]
    cells_here = centre.shape[1]
    widened = extended_2(centre, (("sec", 1),), COLS, False)
    above = widened[:, :cells_here]
    below = widened[:, 2 * COLS :]
    planar = centre.reshape(centre.shape[0], cells_here // COLS, COLS)
    west_cells = jnp.pad(planar[:, :, :-1], ((0, 0), (0, 0), (1, 0))).reshape(centre.shape)
    east_cells = jnp.pad(planar[:, :, 1:], ((0, 0), (0, 0), (0, 1))).reshape(centre.shape)
    summed = extended[2:] + extended[:-2] + above + below + west_cells + east_cells
    return 2.0 * centre - before + stiffness[None, :] * (summed - 6.0 * centre)


def phases(first, second, period_len):
    product = first[:, None] * second[None, :]
    return (product % period_len).astype(jnp.float32) * (two_pi / period_len)


def body(displacement, earlier_field, region_ids, material, mode_shapes, band_edges):
    planes_here = displacement.shape[0]
    period_len = planes_here * lax.axis_size("slab")
    stiffness = lookup_stiffness(region_ids, material)
    current, before = (displacement, earlier_field)
    for _ in range(STEPS):
        extended = extended_2(current, (("slab", 0),), 1, True)
        current, before = (advance(extended, before, stiffness), current)
    modal_part = jnp.dot(current, mode_shapes, precision=lax.Precision.HIGHEST)
    plane_ids = lax.axis_index("slab") * planes_here + jnp.arange(planes_here, dtype=jnp.int32)
    lower_edge = jnp.concatenate([band_edges[0], band_edges[0]])[None, :]
    upper_edge = jnp.concatenate([band_edges[1], band_edges[1]])[None, :]
    empty = jnp.zeros((planes_here, MODES), jnp.float32)
    modal = lax.psum(modal_part, "sec")
    owned_rows = WAVES // lax.axis_size("slab")
    row_count = owned_rows * lax.axis_size("slab")
    block_len = min(row_count, 512)

    def make_one_block(index):
        wavenums = index * block_len + jnp.arange(block_len, dtype=jnp.int32)
        angle = phases(wavenums, plane_ids, period_len)
        return jnp.concatenate(
            [
                jnp.dot(jnp.cos(angle), modal, precision=lax.Precision.HIGHEST),
                jnp.dot(jnp.sin(angle), modal, precision=lax.Precision.HIGHEST),
            ],
            axis=1,
        )

    result = lax.map(make_one_block, jnp.arange(row_count // block_len, dtype=jnp.int32))
    owned = lax.psum_scatter(
        result.reshape(row_count, 2 * MODES), "slab", scatter_dimension=0, tiled=True
    )
    wavenums = (
        lax.axis_index("slab") * owned_rows + jnp.arange(owned.shape[0], dtype=jnp.int32)[:, None]
    )
    in_band = (wavenums >= lower_edge) & (wavenums < upper_edge)
    filtered = jnp.where(in_band, owned, jnp.zeros_like(owned))
    running = empty
    portion = lax.all_gather(filtered, "slab", axis=0, tiled=True)
    row_count = portion.shape[0]
    inverse_block_len = min(row_count, 512)
    portions = portion.reshape(row_count // inverse_block_len, inverse_block_len, 2 * MODES)

    def inverse_one_block(inner, item):
        index, piece_rows = item
        wavenums = index * inverse_block_len + jnp.arange(inverse_block_len, dtype=jnp.int32)
        angle = phases(plane_ids, wavenums, period_len)
        inner = inner + jnp.dot(
            jnp.cos(angle), piece_rows[:, :MODES], precision=lax.Precision.HIGHEST
        )
        inner = inner + jnp.dot(
            jnp.sin(angle), piece_rows[:, MODES:], precision=lax.Precision.HIGHEST
        )
        return (inner, None)

    running, _ = lax.scan(
        inverse_one_block,
        running,
        (jnp.arange(row_count // inverse_block_len, dtype=jnp.int32), portions),
    )
    smooth = running
    smooth = smooth * (2.0 / period_len)
    band_field = jnp.dot(smooth, mode_shapes.T, precision=lax.Precision.HIGHEST).astype(
        jnp.bfloat16
    )
    return (current, band_field)


def solution(mesh):
    return jax.shard_map(
        body,
        mesh=mesh,
        in_specs=(P("slab", "sec"), P("slab", "sec"), P("sec"), P(), P("sec", None), P()),
        out_specs=(P("slab", "sec"), P("slab", "sec")),
        check_vma=False,
    )
```

profile of v0, /device:TPU:32, one launch (start us, length us, event | category | flops | bytes accessed | tf_op | source)
XLA Modules:
  0.0 1638.3 jit_solution(503849871708262057)
XLA Ops:
  10.1 7.5 collective-permute-start.3
  18.4 13.5 collective-permute-start
  31.9 1.9 collective-permute-start.1
  37.0 6.4 collective-permute-done.1
  43.8 1.9 collective-permute-start.6
  45.7 7.5 collective-permute-start.7
  53.3 3.6 collective-permute-start.4
  56.9 2.2 collective-permute-start.5
  59.8 8.8 collective-permute-done.5
  68.9 1.9 collective-permute-start.10
  70.9 7.5 collective-permute-start.11
  78.4 1.9 collective-permute-start.8
  80.4 3.9 collective-permute-start.9
  84.9 6.9 collective-permute-done.9
  92.3 1.9 collective-permute-start.14
  94.2 7.5 collective-permute-start.15
  101.7 1.9 collective-permute-start.12
  103.7 3.9 collective-permute-start.13
  108.2 6.9 collective-permute-done.13
  115.7 18.1 %psum.7 = f32[40,64]{1,0:T(8,128)S(1)} all-reduce(f32[40,64]{1,0:T(8,128)S(1)} %fusion.105), channel_id=1, replica_groups=mesh['slab'=128,'sec'=4] {'sec'}, use_global_device_ids=true, to_apply=%region_1.2 | all-reduce | flops 2560 | bytes 20480 | tf_op jit(solution)/shard_map/psum | solution.py:66
  133.8 41.0 %while.26 = (s32[]{:T(128)}, f32[8,512,128]{2,1,0:T(8,128)}, s32[8]{0:T(128)S(1)}, f32[40,64]{1,0:T(8,128)S(1)}, s32[]{:T(128)}, /*index=5*/s32[]{:T(128)}, s32[1]{0:T(128)}) while((s32[]{:T(128)}, f32[8,512,128]{2,1,0:T(8,128)}, s32[8]{0:T(128)S(1)}, f32[40,64]{1,0:T(8,128)S(1)}, s32[]{:T(128)}, /*index=5*/s32[]{:T(128)}, ...), condition=%wide.region_3.4_spmd.clone, body=%wide.region_2.3_spmd.clone.sunk | while | flops 31892012 | bytes 1862733 | solution.py:82
  175.6 738.4 %reduce-scatter.2.cloned.1.call-done = f32[32,128]{1,0:T(8,128)} async-done(((f32[4096,128]{1,0:T(8,128)}), f32[32,128]{1,0:T(8,128)}) %reduce-scatter.2.cloned.1.call-update) | async-done | bytes 16400 | tf_op jit(solution)/shard_map/reduce_scatter | solution.py:83
  915.5 686.4 %all-gather.2.cloned.1.call-done = f32[4096,128]{1,0:T(8,128)} async-done(((f32[32,128]{1,0:T(8,128)}), f32[4096,128]{1,0:T(8,128)}) %all-gather.2.cloned.1.call-update) | async-done | bytes 2097168 | tf_op jit(solution)/shard_map/all_gather | solution.py:92
  1601.9 28.6 %while.27 = (s32[]{:T(128)}, f32[40,64]{1,0:T(8,128)S(1)}, s32[8]{0:T(128)S(1)}, f32[8,512,128]{2,1,0:T(8,128)}, s32[]{:T(128)}, /*index=5*/s32[]{:T(128)}, s32[1]{0:T(128)}, s32[]{:T(128)}) while((s32[]{:T(128)}, f32[40,64]{1,0:T(8,128)S(1)}, s32[8]{0:T(128)S(1)}, f32[8,512,128]{2,1,0:T(8,128)}, s32[]{:T(128)}, ...), condition=%wide.region_6.7_spmd.clone, body=%wide.region_5.6_spmd.clone.sunk | while | flops 31834156 | bytes 1096291 | solution.py:109
  (187 shorter events, 71.7 us)
Async XLA Ops:
  7.2 108.2 %copy-start = (f32[1024,64]{0,1:T(8,128)S(1)}, f32[1024,64]{0,1:T(8,128)}, u32[]{:S(2)}) copy-start(f32[1024,64]{0,1:T(8,128)} %param.14) | copy-start | bytes 786436
  7.2 36.2 %copy-start.1 = (f32[40,1024]{1,0:T(8,128)S(1)}, f32[40,1024]{1,0:T(8,128)}, u32[]{:S(2)}) copy-start(f32[40,1024]{1,0:T(8,128)} %param.10) | copy-start | bytes 491524
  7.2 36.2 %copy-start.3 = (f32[40,1024]{1,0:T(8,128)S(1)}, f32[40,1024]{1,0:T(8,128)}, u32[]{:S(2)}) copy-start(f32[40,1024]{1,0:T(8,128)} %param.11) | copy-start | bytes 491524
  7.2 906.9 %reduce-scatter.2.cloned.1.call-start = ((), (), s32[]{:S(2)}) async-start(), calls=%async_computation.1 | async-start | bytes 2113536 | tf_op jit(solution)/shard_map/reduce_scatter | solution.py:83
  8.1 35.3 %collective-permute-start.2 = (f32[40,64]{1,0:T(8,128)S(1)}, f32[40,64]{1,0:T(8,128)S(1)}, u32[]{:S(2)}, u32[]{:S(2)}) collective-permute-start(f32[40,64]{1,0:T(8,128)S(1)} %get-tuple-element.212), channel_id=1, source_target_pairs={{0,1},{1,2},{2,3},{4,5},{5,6},{6,7},{8,9},{9,10},{10,11},{12,13},{... | collective-permute-start | bytes 30728 | tf_op jit(solution)/shard_map/ppermute | solution.py:23
  10.1 33.3 %collective-permute-start.3 = (f32[40,64]{1,0:T(8,128)S(1)}, f32[40,64]{1,0:T(8,128)S(1)}, u32[]{:S(2)}, u32[]{:S(2)}) collective-permute-start(f32[40,64]{1,0:T(8,128)S(1)} %get-tuple-element.213), channel_id=1, source_target_pairs={{1,0},{2,1},{3,2},{5,4},{6,5},{7,6},{9,8},{10,9},{11,10},{13,12},{... | collective-permute-start | bytes 30728 | tf_op jit(solution)/shard_map/ppermute | solution.py:24
  18.4 18.6 %collective-permute-start = (f32[1,1024]{1,0:T(1,128)S(1)}, f32[1,1024]{1,0:T(1,128)S(1)}, u32[]{:S(2)}, u32[]{:S(2)}) collective-permute-start(f32[1,1024]{1,0:T(1,128)S(1)} %get-tuple-element.210), channel_id=1, source_target_pairs={{4,0},{8,4},{12,8},{16,12},{20,16},{24,20},{28,24},{32,28},{36,32}... | collective-permute-start | bytes 12296 | tf_op jit(solution)/shard_map/ppermute | solution.py:24
  31.9 11.5 collective-permute-start.1
  43.8 24.8 %collective-permute-start.6 = (f32[40,64]{1,0:T(8,128)S(1)}, f32[40,64]{1,0:T(8,128)S(1)}, u32[]{:S(2)}, u32[]{:S(2)}) collective-permute-start(f32[40,64]{1,0:T(8,128)S(1)} %get-tuple-element.208), channel_id=1, source_target_pairs={{0,1},{1,2},{2,3},{4,5},{5,6},{6,7},{8,9},{9,10},{10,11},{12,13},{... | collective-permute-start | bytes 30728 | tf_op jit(solution)/shard_map/ppermute | solution.py:23
  45.7 22.8 %collective-permute-start.7 = (f32[40,64]{1,0:T(8,128)S(1)}, f32[40,64]{1,0:T(8,128)S(1)}, u32[]{:S(2)}, u32[]{:S(2)}) collective-permute-start(f32[40,64]{1,0:T(8,128)S(1)} %get-tuple-element.209), channel_id=1, source_target_pairs={{1,0},{2,1},{3,2},{5,4},{6,5},{7,6},{9,8},{10,9},{11,10},{13,12},{... | collective-permute-start | bytes 30728 | tf_op jit(solution)/shard_map/ppermute | solution.py:24
  53.3 6.5 collective-permute-start.4
  56.9 11.7 collective-permute-start.5
  68.9 22.9 %collective-permute-start.10 = (f32[40,64]{1,0:T(8,128)S(1)}, f32[40,64]{1,0:T(8,128)S(1)}, u32[]{:S(2)}, u32[]{:S(2)}) collective-permute-start(f32[40,64]{1,0:T(8,128)S(1)} %get-tuple-element.204), channel_id=1, source_target_pairs={{0,1},{1,2},{2,3},{4,5},{5,6},{6,7},{8,9},{9,10},{10,11},{12,13},{... | collective-permute-start | bytes 30728 | tf_op jit(solution)/shard_map/ppermute | solution.py:23
  70.9 21.0 %collective-permute-start.11 = (f32[40,64]{1,0:T(8,128)S(1)}, f32[40,64]{1,0:T(8,128)S(1)}, u32[]{:S(2)}, u32[]{:S(2)}) collective-permute-start(f32[40,64]{1,0:T(8,128)S(1)} %get-tuple-element.205), channel_id=1, source_target_pairs={{1,0},{2,1},{3,2},{5,4},{6,5},{7,6},{9,8},{10,9},{11,10},{13,12},{... | collective-permute-start | bytes 30728 | tf_op jit(solution)/shard_map/ppermute | solution.py:24
  78.4 6.5 collective-permute-start.8
  80.4 11.5 collective-permute-start.9
  92.3 22.9 %collective-permute-start.14 = (f32[40,64]{1,0:T(8,128)S(1)}, f32[40,64]{1,0:T(8,128)S(1)}, u32[]{:S(2)}, u32[]{:S(2)}) collective-permute-start(f32[40,64]{1,0:T(8,128)S(1)} %get-tuple-element.200), channel_id=1, source_target_pairs={{0,1},{1,2},{2,3},{4,5},{5,6},{6,7},{8,9},{9,10},{10,11},{12,13},{... | collective-permute-start | bytes 30728 | tf_op jit(solution)/shard_map/ppermute | solution.py:23
  94.2 21.0 %collective-permute-start.15 = (f32[40,64]{1,0:T(8,128)S(1)}, f32[40,64]{1,0:T(8,128)S(1)}, u32[]{:S(2)}, u32[]{:S(2)}) collective-permute-start(f32[40,64]{1,0:T(8,128)S(1)} %get-tuple-element.201), channel_id=1, source_target_pairs={{1,0},{2,1},{3,2},{5,4},{6,5},{7,6},{9,8},{10,9},{11,10},{13,12},{... | collective-permute-start | bytes 30728 | tf_op jit(solution)/shard_map/ppermute | solution.py:24
  101.7 6.5 collective-permute-start.12
  103.7 11.5 collective-permute-start.13
  115.4 18.4 %copy-start.2 = (f32[40,1024]{1,0:T(8,128)}, f32[40,1024]{1,0:T(8,128)S(1)}, u32[]{:S(2)}) copy-start(f32[40,1024]{1,0:T(8,128)S(1)} %fusion.63) | copy-start | bytes 491524
  174.9 0.7 copy-start.4
  174.9 1427.0 %all-gather.2.cloned.1.call-start = ((), (), s32[]{:S(2)}) async-start(), calls=%async_computation.2 | async-start | bytes 2113536 | tf_op jit(solution)/shard_map/all_gather | solution.py:92
Sparse Core Ops, SparseCore 0:
  175.0 738.9 reduce-scatter.1
  916.7 685.1 all-gather.1
where the time goes:
time: 1640 us
  waiting for transfers between devices  1450 us (88%)
  starting transfers between devices  70.9 us (4%)
  matrix products  34.8 us (2%)
  local copies, waits for them, and re-layouts  30.8 us (2%)
  blocking collectives  18.1 us (1%)
    reduce_scatter x1, waiting for transfers between devices, body(): lax.psum_scatter(result.reshape(row_count, 2 * MODES), 'slab', scatter_di...  738 us
    all_gather x1, waiting for transfers between devices, body(): portion = lax.all_gather(filtered, 'slab', axis=0, tiled=True)  686 us
    ppermute x8, starting transfers between devices, extended_2(): after = lax.ppermute(leading, axis, down)  51.1 us
  transfers between devices with their start and end apart: 18, of which 6 were waited for; matrix products, arithmetic and copies ran while one was open for 0% of the time, Pallas kernels for 0%

commit v1 on v0

--- a/solution.py
+++ b/solution.py
@@ -1,3 +1,4 @@
+import functools
 import math
 import jax
 import jax.numpy as jnp
@@ -11,6 +12,21 @@
 STEPS = 4
 courant_sq = 0.14
 two_pi = 2.0 * math.pi
+
+
+def produce_scales(mine_x, a_name, dim_no):
+    return jnp.concatenate(
+        lax.all_to_all(
+            jnp.stack([mine_x for _ in range(lax.axis_size(a_name))], axis=0),
+            split_axis=0,
+            axis_name=a_name,
+            concat_axis=0,
+        ),
+        dim_no,
+    )
+
+
+clear_boxes_in = functools.partial(produce_scales, a_name="slab", dim_no=0)
 
 
 def extended_2(x, sides, width, wrap):
@@ -89,7 +105,7 @@
     in_band = (wavenums >= lower_edge) & (wavenums < upper_edge)
     filtered = jnp.where(in_band, owned, jnp.zeros_like(owned))
     running = empty
-    portion = lax.all_gather(filtered, "slab", axis=0, tiled=True)
+    portion = clear_boxes_in(filtered)
     row_count = portion.shape[0]
     inverse_block_len = min(row_count, 512)
     portions = portion.reshape(row_count // inverse_block_len, inverse_block_len, 2 * MODES)

time: 1640 us -> 989 us (0.60)
  the two profiles are of different devices: /device:TPU:32 before, /device:TPU:56 now
where the time goes in v1:
time: 989 us; the launch traced here: 988 us
  waiting for transfers between devices  782 us (79%)
  starting transfers between devices  99.5 us (10%)
  matrix products  34.8 us (4%)
  local copies, waits for them, and re-layouts  24.9 us (3%)
  blocking collectives  18.1 us (2%)
  between operations  14.5 us (1%)
  loops' own time  10.4 us (1%)
    reduce_scatter x1, waiting for transfers between devices, body(): lax.psum_scatter(result.reshape(row_count, 2 * MODES), 'slab', scatter_di...  740 us
    ppermute x8, starting transfers between devices, extended_2(): after = lax.ppermute(leading, axis, down)  55.1 us
    all_to_all x1, waiting for transfers between devices, produce_scales(): lax.all_to_all(jnp.stack([mine_x for _ in range(lax.axis_size(a_name))],...  30.9 us
    ppermute x8, starting transfers between devices, extended_2(): before = lax.ppermute(last, axis, up)  23.4 us
    all_to_all x1, starting transfers between devices, produce_scales(): lax.all_to_all(jnp.stack([mine_x for _ in range(lax.axis_size(a_name))],...  21 us
  transfers between devices with their start and end apart: 18, of which 5 were waited for; matrix products, arithmetic and copies ran while one was open for 1% of the time, Pallas kernels for 0%

profile of v1, /device:TPU:56, one launch (start us, length us, event | category | flops | bytes accessed | tf_op | source)
XLA Modules:
  0.0 987.9 jit_solution(2345344725090687751)
XLA Ops:
  10.1 7.5 collective-permute-start.3
  18.4 3.2 collective-permute-start
  21.7 5.3 collective-permute-start.1
  30.6 1.9 collective-permute-start.6
  32.5 7.5 collective-permute-start.7
  40.1 1.9 collective-permute-start.4
  42.0 6.6 collective-permute-start.5
  49.3 5.4 collective-permute-done.5
  55.1 1.9 collective-permute-start.10
  57.0 7.5 collective-permute-start.11
  64.6 9.9 %collective-permute-start.8 = (f32[1,1024]{1,0:T(1,128)S(1)}, f32[1,1024]{1,0:T(1,128)S(1)}, u32[]{:S(2)}, u32[]{:S(2)}) collective-permute-start(f32[1,1024]{1,0:T(1,128)S(1)} %get-tuple-element.202), channel_id=1, source_target_pairs={{4,0},{8,4},{12,8},{16,12},{20,16},{24,20},{28,24},{32,28},{36,32}... | collective-permute-start | bytes 12296 | tf_op jit(solution)/shard_map/ppermute | solution.py:40
  74.5 1.9 collective-permute-start.9
  77.1 2.9 collective-permute-done.9
  80.4 1.9 collective-permute-start.14
  82.3 7.5 collective-permute-start.15
  89.9 9.8 collective-permute-start.12
  99.7 1.9 collective-permute-start.13
  102.2 2.9 collective-permute-done.13
  105.7 18.1 %psum.7 = f32[40,64]{1,0:T(8,128)S(1)} all-reduce(f32[40,64]{1,0:T(8,128)S(1)} %fusion.105), channel_id=1, replica_groups=mesh['slab'=128,'sec'=4] {'sec'}, use_global_device_ids=true, to_apply=%region_1.2 | all-reduce | flops 2560 | bytes 20480 | tf_op jit(solution)/shard_map/psum | solution.py:82
  123.8 39.7 %while.26 = (s32[]{:T(128)}, f32[8,512,128]{2,1,0:T(8,128)}, s32[8]{0:T(128)S(1)}, f32[40,64]{1,0:T(8,128)S(1)}, s32[]{:T(128)}, /*index=5*/s32[]{:T(128)}, s32[1]{0:T(128)}) while((s32[]{:T(128)}, f32[8,512,128]{2,1,0:T(8,128)}, s32[8]{0:T(128)S(1)}, f32[40,64]{1,0:T(8,128)S(1)}, s32[]{:T(128)}, /*index=5*/s32[]{:T(128)}, ...), condition=%wide.region_3.4_spmd.clone, body=%wide.region_2.3_spmd.clone.sunk | while | flops 31892012 | bytes 1862733 | solution.py:98
  164.2 740.0 %reduce-scatter.2.cloned.1.call-done = f32[32,128]{1,0:T(8,128)} async-done(((f32[4096,128]{1,0:T(8,128)}), f32[32,128]{1,0:T(8,128)}) %reduce-scatter.2.cloned.1.call-update) | async-done | bytes 16400 | tf_op jit(solution)/shard_map/reduce_scatter | solution.py:99
  906.7 21.0 %all-to-all-start = ((f32[128,32,128]{2,1,0:T(8,128)}), f32[128,32,128]{2,1,0:T(8,128)S(1)}, u32[]{:S(2)}, u32[]{:S(2)}) async-start(f32[128,32,128]{2,1,0:T(8,128)} %stack.2), calls=%async_computation.1 | async-start | bytes 4194304 | tf_op jit(solution)/shard_map/all_to_all | solution.py:19
  927.7 30.9 %all-to-all-done = f32[128,32,128]{2,1,0:T(8,128)S(1)} async-done(((f32[128,32,128]{2,1,0:T(8,128)}), f32[128,32,128]{2,1,0:T(8,128)S(1)}, u32[]{:S(2)}, u32[]{:S(2)}) %all-to-all-start) | async-done | bytes 2097184 | tf_op jit(solution)/shard_map/all_to_all | solution.py:19
  958.5 21.5 %while.27 = (s32[]{:T(128)}, f32[40,64]{1,0:T(8,128)S(1)}, s32[8]{0:T(128)S(1)}, f32[8,512,128]{2,1,0:T(8,128)S(1)}, s32[]{:T(128)}, /*index=5*/s32[]{:T(128)}, s32[1]{0:T(128)}, s32[]{:T(128)}) while((s32[]{:T(128)}, f32[40,64]{1,0:T(8,128)S(1)}, s32[8]{0:T(128)S(1)}, f32[8,512,128]{2,1,0:T(8,128)S(1)}, s32[]{:T(128)}, ...), condition=%wide.region_6.7_spmd.clone, body=%wide.region_5.6_spmd.clone.sunk | while | flops 31834156 | bytes 1096291 | solution.py:125
  (187 shorter events, 65.1 us)
Async XLA Ops:
  7.2 98.2 %copy-start = (f32[1024,64]{0,1:T(8,128)S(1)}, f32[1024,64]{0,1:T(8,128)}, u32[]{:S(2)}) copy-start(f32[1024,64]{0,1:T(8,128)} %param.14) | copy-start | bytes 786436
  7.2 23.0 %copy-start.1 = (f32[40,1024]{1,0:T(8,128)S(1)}, f32[40,1024]{1,0:T(8,128)}, u32[]{:S(2)}) copy-start(f32[40,1024]{1,0:T(8,128)} %param.10) | copy-start | bytes 491524
  7.2 23.0 %copy-start.3 = (f32[40,1024]{1,0:T(8,128)S(1)}, f32[40,1024]{1,0:T(8,128)}, u32[]{:S(2)}) copy-start(f32[40,1024]{1,0:T(8,128)} %param.11) | copy-start | bytes 491524
  7.2 897.1 %reduce-scatter.2.cloned.1.call-start = ((), (), s32[]{:S(2)}) async-start(), calls=%async_computation.2 | async-start | bytes 2113536 | tf_op jit(solution)/shard_map/reduce_scatter | solution.py:99
  8.1 22.0 %collective-permute-start.2 = (f32[40,64]{1,0:T(8,128)S(1)}, f32[40,64]{1,0:T(8,128)S(1)}, u32[]{:S(2)}, u32[]{:S(2)}) collective-permute-start(f32[40,64]{1,0:T(8,128)S(1)} %get-tuple-element.212), channel_id=1, source_target_pairs={{0,1},{1,2},{2,3},{4,5},{5,6},{6,7},{8,9},{9,10},{10,11},{12,13},{... | collective-permute-start | bytes 30728 | tf_op jit(solution)/shard_map/ppermute | solution.py:39
  10.1 20.1 %collective-permute-start.3 = (f32[40,64]{1,0:T(8,128)S(1)}, f32[40,64]{1,0:T(8,128)S(1)}, u32[]{:S(2)}, u32[]{:S(2)}) collective-permute-start(f32[40,64]{1,0:T(8,128)S(1)} %get-tuple-element.213), channel_id=1, source_target_pairs={{1,0},{2,1},{3,2},{5,4},{6,5},{7,6},{9,8},{10,9},{11,10},{13,12},{... | collective-permute-start | bytes 30728 | tf_op jit(solution)/shard_map/ppermute | solution.py:40
  18.4 11.8 %collective-permute-start = (f32[1,1024]{1,0:T(1,128)S(1)}, f32[1,1024]{1,0:T(1,128)S(1)}, u32[]{:S(2)}, u32[]{:S(2)}) collective-permute-start(f32[1,1024]{1,0:T(1,128)S(1)} %get-tuple-element.210), channel_id=1, source_target_pairs={{4,0},{8,4},{12,8},{16,12},{20,16},{24,20},{28,24},{32,28},{36,32}... | collective-permute-start | bytes 12296 | tf_op jit(solution)/shard_map/ppermute | solution.py:40
  21.7 8.5 collective-permute-start.1
  30.6 24.1 %collective-permute-start.6 = (f32[40,64]{1,0:T(8,128)S(1)}, f32[40,64]{1,0:T(8,128)S(1)}, u32[]{:S(2)}, u32[]{:S(2)}) collective-permute-start(f32[40,64]{1,0:T(8,128)S(1)} %get-tuple-element.208), channel_id=1, source_target_pairs={{0,1},{1,2},{2,3},{4,5},{5,6},{6,7},{8,9},{9,10},{10,11},{12,13},{... | collective-permute-start | bytes 30728 | tf_op jit(solution)/shard_map/ppermute | solution.py:39
  32.5 22.2 %collective-permute-start.7 = (f32[40,64]{1,0:T(8,128)S(1)}, f32[40,64]{1,0:T(8,128)S(1)}, u32[]{:S(2)}, u32[]{:S(2)}) collective-permute-start(f32[40,64]{1,0:T(8,128)S(1)} %get-tuple-element.209), channel_id=1, source_target_pairs={{1,0},{2,1},{3,2},{5,4},{6,5},{7,6},{9,8},{10,9},{11,10},{13,12},{... | collective-permute-start | bytes 30728 | tf_op jit(solution)/shard_map/ppermute | solution.py:40
  40.1 9.2 collective-permute-start.4
  42.0 12.7 %collective-permute-start.5 = (f32[1,1024]{1,0:T(1,128)S(1)}, f32[1,1024]{1,0:T(1,128)S(1)}, u32[]{:S(2)}, u32[]{:S(2)}) collective-permute-start(f32[1,1024]{1,0:T(1,128)S(1)} %get-tuple-element.207), channel_id=1, source_target_pairs={{0,4},{4,8},{8,12},{12,16},{16,20},{20,24},{24,28},{28,32},{32,36}... | collective-permute-start | bytes 12296 | tf_op jit(solution)/shard_map/ppermute | solution.py:39
  55.1 24.9 %collective-permute-start.10 = (f32[40,64]{1,0:T(8,128)S(1)}, f32[40,64]{1,0:T(8,128)S(1)}, u32[]{:S(2)}, u32[]{:S(2)}) collective-permute-start(f32[40,64]{1,0:T(8,128)S(1)} %get-tuple-element.204), channel_id=1, source_target_pairs={{0,1},{1,2},{2,3},{4,5},{5,6},{6,7},{8,9},{9,10},{10,11},{12,13},{... | collective-permute-start | bytes 30728 | tf_op jit(solution)/shard_map/ppermute | solution.py:39
  57.0 23.0 %collective-permute-start.11 = (f32[40,64]{1,0:T(8,128)S(1)}, f32[40,64]{1,0:T(8,128)S(1)}, u32[]{:S(2)}, u32[]{:S(2)}) collective-permute-start(f32[40,64]{1,0:T(8,128)S(1)} %get-tuple-element.205), channel_id=1, source_target_pairs={{1,0},{2,1},{3,2},{5,4},{6,5},{7,6},{9,8},{10,9},{11,10},{13,12},{... | collective-permute-start | bytes 30728 | tf_op jit(solution)/shard_map/ppermute | solution.py:40
  64.6 12.5 %collective-permute-start.8 = (f32[1,1024]{1,0:T(1,128)S(1)}, f32[1,1024]{1,0:T(1,128)S(1)}, u32[]{:S(2)}, u32[]{:S(2)}) collective-permute-start(f32[1,1024]{1,0:T(1,128)S(1)} %get-tuple-element.202), channel_id=1, source_target_pairs={{4,0},{8,4},{12,8},{16,12},{20,16},{24,20},{28,24},{32,28},{36,32}... | collective-permute-start | bytes 12296 | tf_op jit(solution)/shard_map/ppermute | solution.py:40
  74.5 5.5 collective-permute-start.9
  80.4 24.8 %collective-permute-start.14 = (f32[40,64]{1,0:T(8,128)S(1)}, f32[40,64]{1,0:T(8,128)S(1)}, u32[]{:S(2)}, u32[]{:S(2)}) collective-permute-start(f32[40,64]{1,0:T(8,128)S(1)} %get-tuple-element.200), channel_id=1, source_target_pairs={{0,1},{1,2},{2,3},{4,5},{5,6},{6,7},{8,9},{9,10},{10,11},{12,13},{... | collective-permute-start | bytes 30728 | tf_op jit(solution)/shard_map/ppermute | solution.py:39
  82.3 22.8 %collective-permute-start.15 = (f32[40,64]{1,0:T(8,128)S(1)}, f32[40,64]{1,0:T(8,128)S(1)}, u32[]{:S(2)}, u32[]{:S(2)}) collective-permute-start(f32[40,64]{1,0:T(8,128)S(1)} %get-tuple-element.201), channel_id=1, source_target_pairs={{1,0},{2,1},{3,2},{5,4},{6,5},{7,6},{9,8},{10,9},{11,10},{13,12},{... | collective-permute-start | bytes 30728 | tf_op jit(solution)/shard_map/ppermute | solution.py:40
  89.9 12.3 %collective-permute-start.12 = (f32[1,1024]{1,0:T(1,128)S(1)}, f32[1,1024]{1,0:T(1,128)S(1)}, u32[]{:S(2)}, u32[]{:S(2)}) collective-permute-start(f32[1,1024]{1,0:T(1,128)S(1)} %get-tuple-element.198), channel_id=1, source_target_pairs={{4,0},{8,4},{12,8},{16,12},{20,16},{24,20},{28,24},{32,28},{36,32}... | collective-permute-start | bytes 12296 | tf_op jit(solution)/shard_map/ppermute | solution.py:40
  99.7 5.5 collective-permute-start.13
  105.4 18.4 %copy-start.2 = (f32[40,1024]{1,0:T(8,128)}, f32[40,1024]{1,0:T(8,128)S(1)}, u32[]{:S(2)}) copy-start(f32[40,1024]{1,0:T(8,128)S(1)} %fusion.63) | copy-start | bytes 491524
  163.5 0.7 copy-start.4
  906.7 51.9 %all-to-all-start = ((f32[128,32,128]{2,1,0:T(8,128)}), f32[128,32,128]{2,1,0:T(8,128)S(1)}, u32[]{:S(2)}, u32[]{:S(2)}) async-start(f32[128,32,128]{2,1,0:T(8,128)} %stack.2), calls=%async_computation.1 | async-start | bytes 4194304 | tf_op jit(solution)/shard_map/all_to_all | solution.py:19
Sparse Core Ops, SparseCore 0:
  163.6 740.5 reduce-scatter.1
